TPU v7x, 32 devices: a whole 2x2x4 slice. The times are simulated.
32 devices in a mesh: row: 4 (over z), col: 2 (over x), depth: 4 (over y, core).
Axes of the slice: x: 2, y: 2, z: 4, core: 2. Of those that a mesh axis runs over, the one named last changes fastest.
Arguments:
- tokens: bfloat16 [2560, 8192], P(('row', 'depth'), 'col'), may hold values from -6 to 6
- weight: bfloat16 [8192, 4096], P('row', 'col'), may hold values from -0.0625 to 0.0625
- cotangent: bfloat16 [2560, 4096], P(('row', 'depth'), 'col'), may hold values from -6 to 6
- master: float32 [8192, 4096], P(('row', 'depth'), 'col'), may hold values from -0.1 to 0.1
- first_moment: float32 [8192, 4096], P(('row', 'depth'), 'col'), may hold values from -6 to 6
- second_moment: float32 [8192, 4096], P(('row', 'depth'), 'col'), may hold values from 0.1 to 10
Outputs:
- queries: bfloat16 [2560, 4096], P(('row', 'depth'), 'col')
- token_grad: bfloat16 [2560, 8192], P(('row', 'depth'), 'col')
- new_master: float32 [8192, 4096], P(('row', 'depth'), 'col')
- new_first: float32 [8192, 4096], P(('row', 'depth'), 'col')
- new_second: float32 [8192, 4096], P(('row', 'depth'), 'col')
- new_weight: bfloat16 [8192, 4096], P('row', 'col')
All inputs are finite; a program needn't handle non-finite values.
Results may differ from a plain program's by a relative error of at most 0.001.
Values may be sent and summed in bfloat16 or wider, within the bound.
A program may use at most 128 MiB of HBM per device.

v0:
```python
import math
import jax
import jax.numpy as jnp
from jax import lax
from jax.sharding import PartitionSpec as P

beta_one = 0.9
beta_two = 0.95
learn_rate = 0.02
decay_rate = 0.1
adam_eps = 1e-08
bias_one = 1.0 - 0.9**50
bias_two = 1.0 - 0.95**50


def local(tokens, weight, cotangent, master, first_moment, second_moment):
    rows, cols = (lax.axis_size("row"), lax.axis_size("col"))
    block = tokens.shape[0]
    total_tokens = block * rows * lax.axis_size("depth")
    grad_scale = 1.0 / math.sqrt(total_tokens)
    full_rows = lax.all_gather(tokens, "col", axis=1, tiled=True)
    line_cotangent = lax.all_gather(cotangent, "row", axis=0, tiled=True)
    line_tokens = lax.all_to_all(full_rows, "row", split_axis=1, concat_axis=0, tiled=True)
    partial_grad = lax.dot_general(
        line_cotangent, weight, (((1,), (1,)), ((), ())), preferred_element_type=jnp.float32
    )
    piece = lax.psum_scatter(partial_grad, "col", scatter_dimension=1, tiled=True).astype(
        jnp.bfloat16
    )
    partial_queries = jnp.dot(line_tokens, weight, preferred_element_type=jnp.float32)
    queries = lax.psum_scatter(partial_queries, "row", scatter_dimension=0, tiled=True).astype(
        jnp.bfloat16
    )
    piece = lax.all_to_all(
        piece.reshape(rows, block, -1), "row", split_axis=0, concat_axis=0, tiled=True
    )
    piece = lax.all_to_all(
        piece.reshape(cols, rows // cols, block, -1), "col", split_axis=0, concat_axis=0, tiled=True
    )
    token_grad = piece.transpose(2, 1, 0, 3).reshape(tokens.shape)
    token_slab = lax.all_to_all(line_tokens, "depth", split_axis=1, concat_axis=0, tiled=True)
    all_cotangent = lax.all_gather(line_cotangent, "depth", axis=0, tiled=True)
    product = lax.dot_general(
        token_slab, all_cotangent, (((0,), (0,)), ((), ())), preferred_element_type=jnp.float32
    )
    grad = product * grad_scale
    new_first = beta_one * first_moment + (1.0 - beta_one) * grad
    new_second = beta_two * second_moment + (1.0 - beta_two) * grad * grad
    step_value = new_first / bias_one / (jnp.sqrt(new_second / bias_two) + adam_eps)
    new_master = master - learn_rate * (step_value + decay_rate * master)
    shard_weight = new_master.astype(jnp.bfloat16)
    new_weight = lax.all_gather(shard_weight, "depth", axis=0, tiled=True)
    return (queries, token_grad, new_master, new_first, new_second, new_weight)


def solution(mesh):
    in_specs = (
        P(("row", "depth"), "col"),
        P("row", "col"),
        P(("row", "depth"), "col"),
        P(("row", "depth"), "col"),
        P(("row", "depth"), "col"),
        P(("row", "depth"), "col"),
    )
    out_specs = (
        P(("row", "depth"), "col"),
        P(("row", "depth"), "col"),
        P(("row", "depth"), "col"),
        P(("row", "depth"), "col"),
        P(("row", "depth"), "col"),
        P("row", "col"),
    )
    return jax.shard_map(local, mesh=mesh, in_specs=in_specs, out_specs=out_specs, check_vma=False)
```

profile of v0, /device:TPU:0, one launch (start us, length us, event | category | flops | bytes accessed | tf_op | source)
XLA Modules:
  0.0 441.7 jit_solution(11255023881615150435)
XLA Ops:
  7.2 0.0 all-gather.7.cloned.1.call-start
  7.2 0.7 all-gather.7.cloned.1.call-update
  7.9 0.0 all-gather.5.cloned.1.call-start
  7.9 0.7 all-gather.5.cloned.1.call-update
  8.6 0.0 all-gather.9.cloned.1.call-start
  8.7 58.3 %all-gather.7.cloned.1.call-done = bf16[640,2048]{1,0:T(8,128)(2,1)} async-done(((bf16[160,2048]{1,0:T(8,128)(2,1)}), bf16[640,2048]{1,0:T(8,128)(2,1)}) %all-gather.7.cloned.1.call-update) | async-done | bytes 2621456 | tf_op jit(solution)/shard_map/all_gather | solution.py:22
  67.0 0.0 all-gather.9.cloned.1.call-update
  67.1 0.0 reduce-scatter.5.cloned.1.call-start
  67.1 11.1 %fusion.2 = f32[640,2048]{1,0:T(8,128)} fusion(bf16[640,2048]{1,0:T(8,128)(2,1)} %all-gather.7.cloned.1.call-done, bf16[2048,2048]{1,0:T(8,128)(2,1)} %param.7), kind=kOutput, calls=%fused_computation.6 | convolution fusion | flops 5368709120 | bytes 16252928 | tf_op jit(solution)/shard_map/dot_general | solution.py:24
  78.2 0.0 reduce-scatter.5.cloned.1.call-update
  78.2 0.0 reduce-scatter.3.cloned.1.call-start
  78.3 28.1 %all-gather.5.cloned.1.call-done = bf16[160,8192]{1,0:T(8,128)(2,1)} async-done(((bf16[160,4096]{1,0:T(8,128)(2,1)}), bf16[160,8192]{1,0:T(8,128)(2,1)}) %all-gather.5.cloned.1.call-update) | async-done | bytes 2621456 | tf_op jit(solution)/shard_map/all_gather | solution.py:21
  106.4 2.1 copy.27
  108.4 63.7 %all_to_all.48 = bf16[160,4,2048]{2,0,1:T(8,128)(2,1)S(1)} all-to-all(bf16[160,4,2048]{2,0,1:T(8,128)(2,1)S(1)} %bitcast.21), channel_id=1, replica_groups=mesh['row'=4,'col'=2,'depth'=4] {'row'}, dimensions={1} | all-to-all | bytes 5242880 | tf_op jit(solution)/shard_map/all_to_all | solution.py:23
  172.1 9.4 %fusion.1 = f32[640,2048]{1,0:T(8,128)} fusion(bf16[640,2048]{1,0:T(8,128)(2,1)S(1)} %bitcast.19, bf16[2048,2048]{1,0:T(8,128)(2,1)} %param.7), kind=kOutput, calls=%fused_computation.5 | convolution fusion | flops 5368709120 | bytes 16252928 | tf_op jit(solution)/shard_map/dot_general | solution.py:30
  181.5 0.0 reduce-scatter.3.cloned.1.call-update
  181.6 0.0 all-gather.11.cloned.1.call-start
  181.6 3.5 all_to_all.40
  185.2 2.9 copy.24
  188.1 33.8 %all_to_all.49 = bf16[640,4,512]{2,0,1:T(8,128)(2,1)S(1)} all-to-all(bf16[640,4,512]{2,0,1:T(8,128)(2,1)S(1)} %copy.24), channel_id=1, replica_groups=mesh['row'=4,'col'=2,'depth'=4] {'depth'}, dimensions={1} | all-to-all | bytes 5242880 | tf_op jit(solution)/shard_map/all_to_all | solution.py:41
  221.8 0.0 all-gather.9.cloned.1.call-done
  221.9 18.4 %fusion = (bf16[512,2048]{1,0:T(8,128)(2,1)}, f32[512,2048]{1,0:T(8,128)}, f32[512,2048]{1,0:T(8,128)}, f32[512,2048]{1,0:T(8,128)}) fusion(f32[512,2048]{1,0:T(8,128)} %param.9, f32[512,2048]{1,0:T(8,128)} %param.10, f32[512,2048]{1,0:T(8,128)} %param.11, bf16[2560,512]{1,0:T(8,128)(2,1)S(1)} %bitcast.26, bf16[2560,2048]{1,0:T(8,128)(2,1)} %all-gather.9.cloned.1.call-done), kind=kOutput, calls=%fused_computation.4 | convolution fusion | flops 5386534912 | bytes 40370176 | tf_op jit(solution)/shard_map/dot_general | solution.py:43
  240.3 0.0 all-gather.11.cloned.1.call-update
  240.3 5.8 %reduce-scatter.5.cloned.1.call-done = f32[640,1024]{1,0:T(8,128)} async-done(((f32[640,2048]{1,0:T(8,128)}), f32[640,1024]{1,0:T(8,128)}) %reduce-scatter.5.cloned.1.call-update) | async-done | bytes 2621456 | tf_op jit(solution)/shard_map/reduce_scatter | solution.py:27
  246.1 1.9 convert_element_type.10
  248.0 70.7 %all_to_all.50 = bf16[4,160,1024]{2,1,0:T(8,128)(2,1)S(1)} all-to-all(bf16[4,160,1024]{2,1,0:T(8,128)(2,1)S(1)} %bitcast.24), channel_id=1, replica_groups=mesh['row'=4,'col'=2,'depth'=4] {'row'}, dimensions={0} | all-to-all | bytes 2621440 | tf_op jit(solution)/shard_map/all_to_all | solution.py:34
  318.7 1.3 copy.22
  320.1 13.3 %all_to_all.51 = bf16[2,2,160,1024]{3,1,2,0:T(2,128)(2,1)S(1)} all-to-all(bf16[2,2,160,1024]{3,1,2,0:T(2,128)(2,1)S(1)} %copy.22), channel_id=1, replica_groups=mesh['row'=4,'col'=2,'depth'=4] {'col'}, dimensions={0} | all-to-all | bytes 2621440 | tf_op jit(solution)/shard_map/all_to_all | solution.py:37
  333.3 2.0 copy.23
  335.4 1.8 reshape.30
  337.2 24.3 %reduce-scatter.3.cloned.1.call-done = f32[160,2048]{1,0:T(8,128)} async-done(((f32[640,2048]{1,0:T(8,128)}), f32[160,2048]{1,0:T(8,128)}) %reduce-scatter.3.cloned.1.call-update) | async-done | bytes 1310736 | tf_op jit(solution)/shard_map/reduce_scatter | solution.py:31
  361.5 2.2 convert_element_type.9
  363.8 62.7 %all-gather.11.cloned.1.call-done = bf16[2048,2048]{1,0:T(8,128)(2,1)} async-done(((bf16[512,2048]{1,0:T(8,128)(2,1)}), bf16[2048,2048]{1,0:T(8,128)(2,1)}) %all-gather.11.cloned.1.call-update) | async-done | bytes 8388624 | tf_op jit(solution)/shard_map/all_gather | solution.py:52
  426.4 8.4 %copy.29 = bf16[2048,2048]{1,0:T(8,128)(2,1)} copy(bf16[2048,2048]{1,0:T(8,128)(2,1)} %all-gather.11.cloned.1.call-done) | data formatting | bytes 16777216
Async XLA Ops:
  7.2 59.9 %all-gather.7.cloned.1.call-start = ((), (), s32[]{:S(2)}) async-start(), calls=%async_computation.8 | async-start | bytes 3276800 | tf_op jit(solution)/shard_map/all_gather | solution.py:22
  7.9 98.5 %all-gather.5.cloned.1.call-start = ((), (), s32[]{:S(2)}) async-start(), calls=%async_computation.6 | async-start | bytes 3932160 | tf_op jit(solution)/shard_map/all_gather | solution.py:21
  8.6 213.2 %all-gather.9.cloned.1.call-start = ((), (), s32[]{:S(2)}) async-start(), calls=%async_computation.10 | async-start | bytes 13107200 | tf_op jit(solution)/shard_map/all_gather | solution.py:42
  67.1 179.0 %reduce-scatter.5.cloned.1.call-start = ((), (), s32[]{:S(2)}) async-start(), calls=%async_computation.9 | async-start | bytes 7864320 | tf_op jit(solution)/shard_map/reduce_scatter | solution.py:27
  78.2 283.3 %reduce-scatter.3.cloned.1.call-start = ((), (), s32[]{:S(2)}) async-start(), calls=%async_computation.7 | async-start | bytes 6553600 | tf_op jit(solution)/shard_map/reduce_scatter | solution.py:31
  181.6 244.9 %all-gather.11.cloned.1.call-start = ((), (), s32[]{:S(2)}) async-start(), calls=%async_computation.11 | async-start | bytes 10485760 | tf_op jit(solution)/shard_map/all_gather | solution.py:52
Sparse Core Ops, SparseCore 0:
  9.5 57.4 all-gather.6
  68.6 37.7 all-gather.4
  107.9 70.1 all-gather.8
  180.3 65.7 reduce-scatter.4
  248.8 112.6 reduce-scatter.2
  362.9 63.4 all-gather.10
where the time goes:
time: 442 us
  waiting for transfers between devices  181 us (41%)
  blocking collectives  181 us (41%)
  matrix products  39 us (9%)
  local copies, waits for them, and re-layouts  22.1 us (5%)
  between operations  14.1 us (3%)
    all_to_all x1, blocking collectives, local(): lax.all_to_all(piece.reshape(rows, block, -1), 'row', split_axis=0, conca...  70.7 us
    all_to_all x1, blocking collectives, local(): lax.all_to_all(full_rows, 'row', split_axis=1, concat_axis=0, tiled=True)  63.7 us
    all_gather x1, waiting for transfers between devices, local(): new_weight = lax.all_gather(shard_weight, 'depth', axis=0, tiled=True)  62.7 us
    all_gather x1, waiting for transfers between devices, local(): line_cotangent = lax.all_gather(cotangent, 'row', axis=0, tiled=True)  58.3 us
    all_to_all x1, blocking collectives, local(): lax.all_to_all(line_tokens, 'depth', split_axis=1, concat_axis=0, tiled=T...  33.8 us
    all_gather x1, waiting for transfers between devices, local(): full_rows = lax.all_gather(tokens, 'col', axis=1, tiled=True)  28.1 us
    reduce_scatter x1, waiting for transfers between devices, local(): lax.psum_scatter(partial_queries, 'row', scatter_dimension=0, tiled=True)  24.3 us
    dot_general x1, matrix products, local(): lax.dot_general(token_slab, all_cotangent, (((0,), (0,)), ((), ())), pref...  18.4 us
  transfers between devices with their start and end apart: 6, of which 5 were waited for; matrix products, arithmetic and copies ran while one was open for 12% of the time, Pallas kernels for 0%

commit v1 on v0

--- a/solution.py
+++ b/solution.py
@@ -13,13 +13,24 @@
 bias_two = 1.0 - 0.95**50
 
 
+def pass_along(x, axis, dim):
+    peers = lax.axis_size(axis)
+    forward = [(i, (i + 1) % peers) for i in range(peers)]
+    shards = [x]
+    for far in range(1, peers):
+        shards = [lax.ppermute(shards[0], axis, forward), *shards]
+    full = jnp.concatenate(shards, axis=dim)
+    places = (lax.axis_index(axis) + 1) * shards[-1].shape[dim]
+    return jnp.roll(full, places, axis=dim)
+
+
 def local(tokens, weight, cotangent, master, first_moment, second_moment):
     rows, cols = (lax.axis_size("row"), lax.axis_size("col"))
     block = tokens.shape[0]
     total_tokens = block * rows * lax.axis_size("depth")
     grad_scale = 1.0 / math.sqrt(total_tokens)
     full_rows = lax.all_gather(tokens, "col", axis=1, tiled=True)
-    line_cotangent = lax.all_gather(cotangent, "row", axis=0, tiled=True)
+    line_cotangent = pass_along(cotangent, "row", 0)
     line_tokens = lax.all_to_all(full_rows, "row", split_axis=1, concat_axis=0, tiled=True)
     partial_grad = lax.dot_general(
         line_cotangent, weight, (((1,), (1,)), ((), ())), preferred_element_type=jnp.float32

time: 442 us -> 425 us (0.962)
  local copies, waits for them, and re-layouts: 22.1 us -> 62.4 us
  blocking collectives: 181 us -> 148 us
  waiting for transfers between devices: 181 us -> 150 us
  starting transfers between devices: 0.24 us -> 7.15 us
    all_gather x1 -> x0, waiting for transfers between devices: 58.3 us -> none  [local(): line_cotangent = lax.all_gather(cotangent, 'row', axis=0, tiled=True)]
    ppermute x0 -> x3, waiting for transfers between devices: none -> 51.4 us  [pass_along(): shards = [lax.ppermute(shards[0], axis, forward), *shards]]
    unnamed x1 -> x16, local copies, waits for them, and re-layouts: 8.44 us -> 45.1 us
    all_to_all x1 -> x0, blocking collectives: 33.8 us -> none  [local(): lax.all_to_all(line_tokens, 'depth', split_axis=1, concat_axis=0, tiled=T...]
    all_gather x1, waiting for transfers between devices: 28.1 us -> 9.71 us  [local(): full_rows = lax.all_gather(tokens, 'col', axis=1, tiled=True)]
    all_gather x1, waiting for transfers between devices: 62.7 us -> 46.2 us  [local(): new_weight = lax.all_gather(shard_weight, 'depth', axis=0, tiled=True)]
    all_to_all x0 -> x1, waiting for transfers between devices: none -> 14.8 us  [local(): lax.all_to_all(line_tokens, 'depth', split_axis=1, concat_axis=0, tiled=T...]
  transfers between devices with their start and end apart: 6 -> 9, of which waited for: 5 -> 8; matrix products, arithmetic and copies ran while one was open for 12% -> 21% of each run, Pallas kernels for 0% -> 0%
where the time goes in v1:
time: 425 us; the launch traced here: 424 us
  waiting for transfers between devices  150 us (35%)
  blocking collectives  148 us (35%)
  local copies, waits for them, and re-layouts  62.4 us (15%)
  matrix products  39.5 us (9%)
  between operations  13.9 us (3%)
  starting transfers between devices  7.15 us (2%)
    all_to_all x1, blocking collectives, local(): lax.all_to_all(piece.reshape(rows, block, -1), 'row', split_axis=0, conca...  70.7 us
    all_to_all x1, blocking collectives, local(): lax.all_to_all(full_rows, 'row', split_axis=1, concat_axis=0, tiled=True)  63.7 us
    ppermute x3, waiting for transfers between devices, pass_along(): shards = [lax.ppermute(shards[0], axis, forward), *shards]  51.4 us
    all_gather x1, waiting for transfers between devices, local(): new_weight = lax.all_gather(shard_weight, 'depth', axis=0, tiled=True)  46.2 us
    unnamed x16, local copies, waits for them, and re-layouts  45.1 us
    reduce_scatter x1, waiting for transfers between devices, local(): lax.psum_scatter(partial_queries, 'row', scatter_dimension=0, tiled=True)  24.3 us
    dot_general x1, matrix products, local(): lax.dot_general(token_slab, all_cotangent, (((0,), (0,)), ((), ())), pref...  18.9 us
    all_to_all x1, waiting for transfers between devices, local(): lax.all_to_all(line_tokens, 'depth', split_axis=1, concat_axis=0, tiled=T...  14.8 us
  transfers between devices with their start and end apart: 9, of which 8 were waited for; matrix products, arithmetic and copies ran while one was open for 21% of the time, Pallas kernels for 0%

profile of v1, /device:TPU:0, one launch (start us, length us, event | category | flops | bytes accessed | tf_op | source)
XLA Modules:
  0.0 424.3 jit_solution(10655208818585960207)
XLA Ops:
  7.2 0.0 copy-start
  7.2 0.0 all-gather.4.cloned.1.call-start
  7.2 3.1 collective-permute-start
  10.3 17.0 %collective-permute-done = bf16[160,2048]{1,0:T(8,128)(2,1)S(1)} collective-permute-done((bf16[160,2048]{1,0:T(8,128)(2,1)}, bf16[160,2048]{1,0:T(8,128)(2,1)S(1)}, u32[]{:S(2)}, u32[]{:S(2)}) %collective-permute-start) | collective-permute-done | bytes 655392 | tf_op jit(solution)/shard_map/ppermute | solution.py:21
  27.3 0.0 collective-permute-start.1
  27.3 17.7 %collective-permute-done.1 = bf16[160,2048]{1,0:T(8,128)(2,1)S(1)} collective-permute-done((bf16[160,2048]{1,0:T(8,128)(2,1)S(1)}, bf16[160,2048]{1,0:T(8,128)(2,1)S(1)}, u32[]{:S(2)}, u32[]{:S(2)}) %collective-permute-start.1) | collective-permute-done | bytes 655392 | tf_op jit(solution)/shard_map/ppermute | solution.py:21
  45.0 0.0 collective-permute-start.2
  45.0 0.0 all-gather.4.cloned.1.call-update
  45.0 0.0 all-gather.6.cloned.1.call-start
  45.1 16.7 %collective-permute-done.2 = bf16[160,2048]{1,0:T(8,128)(2,1)S(1)} collective-permute-done((bf16[160,2048]{1,0:T(8,128)(2,1)S(1)}, bf16[160,2048]{1,0:T(8,128)(2,1)S(1)}, u32[]{:S(2)}, u32[]{:S(2)}) %collective-permute-start.2) | collective-permute-done | bytes 655392 | tf_op jit(solution)/shard_map/ppermute | solution.py:21
  62.0 0.0 copy-done
  62.3 2.2 constant_dynamic-slice_fusion
  64.5 0.0 all-gather.6.cloned.1.call-update
  64.5 0.0 reduce-scatter.5.cloned.1.call-start
  64.5 11.1 %fusion.2 = f32[640,2048]{1,0:T(8,128)} fusion(bf16[640,2048]{1,0:T(8,128)(2,1)} %constant_dynamic-slice_fusion, bf16[2048,2048]{1,0:T(8,128)(2,1)} %param.7), kind=kOutput, calls=%fused_computation.15 | convolution fusion | flops 5368709120 | bytes 16252928 | tf_op jit(solution)/shard_map/dot_general | solution.py:35
  75.6 0.0 reduce-scatter.5.cloned.1.call-update
  75.7 0.0 reduce-scatter.3.cloned.1.call-start
  75.7 9.7 %all-gather.4.cloned.1.call-done = bf16[160,8192]{1,0:T(8,128)(2,1)} async-done(((bf16[160,4096]{1,0:T(8,128)(2,1)}), bf16[160,8192]{1,0:T(8,128)(2,1)}) %all-gather.4.cloned.1.call-update) | async-done | bytes 2621456 | tf_op jit(solution)/shard_map/all_gather | solution.py:32
  85.4 2.1 copy.67
  87.5 63.7 %all_to_all.48 = bf16[160,4,2048]{2,0,1:T(8,128)(2,1)S(1)} all-to-all(bf16[160,4,2048]{2,0,1:T(8,128)(2,1)S(1)} %bitcast.27), channel_id=1, replica_groups=mesh['row'=4,'col'=2,'depth'=4] {'row'}, dimensions={1} | all-to-all | bytes 5242880 | tf_op jit(solution)/shard_map/all_to_all | solution.py:34
  151.1 9.4 %fusion.1 = f32[640,2048]{1,0:T(8,128)} fusion(bf16[640,2048]{1,0:T(8,128)(2,1)S(1)} %bitcast.25, bf16[2048,2048]{1,0:T(8,128)(2,1)} %param.7), kind=kOutput, calls=%fused_computation.14 | convolution fusion | flops 5368709120 | bytes 16252928 | tf_op jit(solution)/shard_map/dot_general | solution.py:41
  160.6 0.0 reduce-scatter.3.cloned.1.call-update
  160.6 3.5 all_to_all.40
  164.1 4.2 copy.57
  168.3 3.7 all-to-all-start.3
  172.0 0.2 all-gather.8.cloned.1.call-start
  172.2 5.3 %copy.60 = f32[512,2048]{0,1:T(8,128)} copy(f32[512,2048]{1,0:T(8,128)} %param.9) | data formatting | bytes 8388608 | tf_op args[3]
  177.6 5.3 %copy.56 = f32[512,2048]{0,1:T(8,128)} copy(f32[512,2048]{1,0:T(8,128)} %param.10) | data formatting | bytes 8388608 | tf_op args[4]
  182.9 5.5 %copy.58 = f32[512,2048]{0,1:T(8,128)} copy(f32[512,2048]{1,0:T(8,128)} %param.11) | data formatting | bytes 8388608 | tf_op args[5]
  188.4 14.8 %all-to-all-done.3 = bf16[640,4,512]{2,0,1:T(8,128)(2,1)S(1)} async-done(((bf16[640,4,512]{2,0,1:T(8,128)(2,1)}), bf16[640,4,512]{2,0,1:T(8,128)(2,1)S(1)}, u32[]{:S(2)}, u32[]{:S(2)}) %all-to-all-start.3) | async-done | bytes 2621472 | tf_op jit(solution)/shard_map/all_to_all | solution.py:52
  203.3 0.0 all-gather.6.cloned.1.call-done
  203.3 18.9 %fusion = (bf16[512,2048]{0,1:T(8,128)(2,1)}, f32[512,2048]{0,1:T(8,128)}, f32[512,2048]{0,1:T(8,128)}, f32[512,2048]{0,1:T(8,128)}) fusion(f32[512,2048]{0,1:T(8,128)} %copy.60, f32[512,2048]{0,1:T(8,128)} %copy.56, f32[512,2048]{0,1:T(8,128)} %copy.58, bf16[2560,2048]{1,0:T(8,128)(2,1)} %all-gather.6.cloned.1.call-done, bf16[2560,512]{1,0:T(8,128)(2,1)S(1)} %bitcast.32), kind=kOutput, calls=%fused_computation.13 | convolution fusion | flops 5386534912 | bytes 40370176 | tf_op jit(solution)/shard_map/dot_general | solution.py:54
  222.2 0.0 all-gather.8.cloned.1.call-update
  222.2 3.1 reduce-scatter.5.cloned.1.call-done
  225.3 1.9 convert_element_type.10
  227.2 70.7 %all_to_all.49 = bf16[4,160,1024]{2,1,0:T(8,128)(2,1)S(1)} all-to-all(bf16[4,160,1024]{2,1,0:T(8,128)(2,1)S(1)} %bitcast.30), channel_id=1, replica_groups=mesh['row'=4,'col'=2,'depth'=4] {'row'}, dimensions={0} | all-to-all | bytes 2621440 | tf_op jit(solution)/shard_map/all_to_all | solution.py:45
  297.9 1.3 copy.54
  299.2 13.3 %all_to_all.50 = bf16[2,2,160,1024]{3,1,2,0:T(2,128)(2,1)S(1)} all-to-all(bf16[2,2,160,1024]{3,1,2,0:T(2,128)(2,1)S(1)} %copy.54), channel_id=1, replica_groups=mesh['row'=4,'col'=2,'depth'=4] {'col'}, dimensions={0} | all-to-all | bytes 2621440 | tf_op jit(solution)/shard_map/all_to_all | solution.py:48
  312.5 2.0 copy.55
  314.6 1.8 reshape.30
  316.4 24.3 %reduce-scatter.3.cloned.1.call-done = f32[160,2048]{1,0:T(8,128)} async-done(((f32[640,2048]{1,0:T(8,128)}), f32[160,2048]{1,0:T(8,128)}) %reduce-scatter.3.cloned.1.call-update) | async-done | bytes 1310736 | tf_op jit(solution)/shard_map/reduce_scatter | solution.py:42
  340.7 2.2 convert_element_type.9
  342.9 5.3 %copy.61 = f32[512,2048]{1,0:T(8,128)} copy(f32[512,2048]{0,1:T(8,128)} %get-tuple-element.37) | data formatting | bytes 8388608
  348.3 5.3 %copy.62 = f32[512,2048]{1,0:T(8,128)} copy(f32[512,2048]{0,1:T(8,128)} %get-tuple-element.38) | data formatting | bytes 8388608
  353.6 5.7 %copy.63 = f32[512,2048]{1,0:T(8,128)} copy(f32[512,2048]{0,1:T(8,128)} %get-tuple-element.39) | data formatting | bytes 8388608
  359.4 46.2 %all-gather.8.cloned.1.call-done = bf16[2048,2048]{0,1:T(8,128)(2,1)} async-done(((bf16[512,2048]{0,1:T(8,128)(2,1)}), bf16[2048,2048]{0,1:T(8,128)(2,1)}) %all-gather.8.cloned.1.call-update) | async-done | bytes 8388624 | tf_op jit(solution)/shard_map/all_gather | solution.py:63
  405.6 12.2 %copy.64 = bf16[2048,2048]{1,0:T(8,128)(2,1)} copy(bf16[2048,2048]{0,1:T(8,128)(2,1)} %all-gather.8.cloned.1.call-done) | data formatting | bytes 16777216
  (8 shorter events, 0.4 us)
Async XLA Ops:
  7.2 54.8 %copy-start = (bf16[160,2048]{1,0:T(8,128)(2,1)S(1)}, bf16[160,2048]{1,0:T(8,128)(2,1)}, u32[]{:S(2)}) copy-start(bf16[160,2048]{1,0:T(8,128)(2,1)} %param.8) | copy-start | bytes 1966084
  7.2 78.2 %all-gather.4.cloned.1.call-start = ((), (), s32[]{:S(2)}) async-start(), calls=%async_computation.6 | async-start | bytes 3932160 | tf_op jit(solution)/shard_map/all_gather | solution.py:32
  7.2 20.1 %collective-permute-start = (bf16[160,2048]{1,0:T(8,128)(2,1)}, bf16[160,2048]{1,0:T(8,128)(2,1)S(1)}, u32[]{:S(2)}, u32[]{:S(2)}) collective-permute-start(bf16[160,2048]{1,0:T(8,128)(2,1)} %param.8), channel_id=1, source_target_pairs={{0,8},{8,16},{16,24},{24,0},{1,9},{9,17},{17,25},{25,1},{2,10},{10... | collective-permute-start | bytes 1966088 | tf_op jit(solution)/shard_map/ppermute | solution.py:21
  27.3 17.7 %collective-permute-start.1 = (bf16[160,2048]{1,0:T(8,128)(2,1)S(1)}, bf16[160,2048]{1,0:T(8,128)(2,1)S(1)}, u32[]{:S(2)}, u32[]{:S(2)}) collective-permute-start(bf16[160,2048]{1,0:T(8,128)(2,1)S(1)} %collective-permute-done), channel_id=1, source_target_pairs={{0,8},{8,16},{16,24},{24,0},{1,9},{9,17},{17,25},{25,1},{2,10},{10... | collective-permute-start | bytes 1966088 | tf_op jit(solution)/shard_map/ppermute | solution.py:21
  45.0 16.8 %collective-permute-start.2 = (bf16[160,2048]{1,0:T(8,128)(2,1)S(1)}, bf16[160,2048]{1,0:T(8,128)(2,1)S(1)}, u32[]{:S(2)}, u32[]{:S(2)}) collective-permute-start(bf16[160,2048]{1,0:T(8,128)(2,1)S(1)} %collective-permute-done.1), channel_id=1, source_target_pairs={{0,8},{8,16},{16,24},{24,0},{1,9},{9,17},{17,25},{25,1},{2,10},{10... | collective-permute-start | bytes 1966088 | tf_op jit(solution)/shard_map/ppermute | solution.py:21
  45.0 158.2 %all-gather.6.cloned.1.call-start = ((), (), s32[]{:S(2)}) async-start(), calls=%async_computation.9 | async-start | bytes 13107200 | tf_op jit(solution)/shard_map/all_gather | solution.py:53
  64.5 160.8 %reduce-scatter.5.cloned.1.call-start = ((), (), s32[]{:S(2)}) async-start(), calls=%async_computation.8 | async-start | bytes 7864320 | tf_op jit(solution)/shard_map/reduce_scatter | solution.py:38
  75.7 265.1 %reduce-scatter.3.cloned.1.call-start = ((), (), s32[]{:S(2)}) async-start(), calls=%async_computation.7 | async-start | bytes 6553600 | tf_op jit(solution)/shard_map/reduce_scatter | solution.py:42
  168.3 34.9 %all-to-all-start.3 = ((bf16[640,4,512]{2,0,1:T(8,128)(2,1)}), bf16[640,4,512]{2,0,1:T(8,128)(2,1)S(1)}, u32[]{:S(2)}, u32[]{:S(2)}) async-start(bf16[640,4,512]{2,0,1:T(8,128)(2,1)} %copy.57), calls=%async_computation.5 | async-start | bytes 5242880 | tf_op jit(solution)/shard_map/all_to_all | solution.py:52
  172.0 233.6 %all-gather.8.cloned.1.call-start = ((), (), s32[]{:S(2)}) async-start(), calls=%async_computation.10 | async-start | bytes 10485760 | tf_op jit(solution)/shard_map/all_gather | solution.py:63
Sparse Core Ops, SparseCore 0:
  45.1 40.2 all-gather.3
  87.0 70.1 all-gather.5
  159.5 65.7 reduce-scatter.4
  228.0 112.6 reduce-scatter.2
  342.1 63.4 all-gather.7
